TPU v7x, 32 devices: a whole 2x2x4 slice. The times are simulated.
32 devices in a mesh: row: 16 (over z, y, x), col: 2 (over core).
Axes of the slice: x: 2, y: 2, z: 4, core: 2. Of those that a mesh axis runs over, the one named last changes fastest.
Arguments:
- samples: bfloat16 [32768, 8192], P('row', 'col'), may hold values from -0.046875 to 0.046875
- targets: float32 [32768, 128], P('row'), may hold values from -6 to 6
- factor_inv: float32 [2, 4096, 4096], P('col', None, 'row'), may hold values from -1 to 1, as said below
Outputs:
- solution: float32 [8192, 128], P('col')
- residual: float32 [32768, 128], P('row')
Inputs may be any that keep to these rules, and one draw needn't show every extreme that they name: Each factor_inv[j] is lower triangular with a positive diagonal.
All inputs are finite; a program needn't handle non-finite values.
Results may differ from a plain program's by a relative error of at most 0.0039.
Values sent between devices are 32-bit elements; how exact they have to be, the bound alone decides.
A program may use at most 128 MiB of HBM per device.

v0:
```python
import jax
import jax.numpy as jnp
from jax import lax
from jax.sharding import PartitionSpec as P

ROUNDS = 3


ridge_weight = 0.5


def run_group(samples, residual, inverse, own_rows, offset, relaxation):
    solution = jnp.zeros((samples.shape[1], residual.shape[1]), jnp.float32)
    for sweep in range(ROUNDS):
        res16 = residual.astype(jnp.bfloat16)
        part_grad = jnp.einsum("rb,rk->bk", samples, res16, preferred_element_type=jnp.float32)
        own_solution = lax.dynamic_slice_in_dim(solution, offset, own_rows, 0)
        grad_total = lax.psum(part_grad, "row")
        grad_own = (
            lax.dynamic_slice_in_dim(grad_total, offset, own_rows, 0) - ridge_weight * own_solution
        )
        term = jnp.dot(inverse, grad_own, precision=lax.Precision.HIGHEST)
        image = lax.psum(term, "row")
        update_own = jnp.einsum("bc,bk->ck", inverse, image, precision=lax.Precision.HIGHEST)
        update = lax.all_gather(update_own, "row", axis=0, tiled=True)
        solution = solution + relaxation * update
        change = jnp.dot(samples, update.astype(jnp.bfloat16), preferred_element_type=jnp.float32)
        residual = residual - relaxation * lax.psum(change, "col")
    return (solution, residual)


def per_device(samples, targets, factor_inv):
    inverse = factor_inv[0]
    own_rows = inverse.shape[1]
    offset = lax.axis_index("row") * own_rows
    relaxation = 1.0 / lax.axis_size("col")
    solution, residual = run_group(samples, targets, inverse, own_rows, offset, relaxation)
    return (solution, residual)


def solution(mesh):
    in_specs = (P("row", "col"), P("row", None), P("col", None, "row"))
    out_specs = (P("col", None), P("row", None))
    return jax.shard_map(
        per_device, mesh=mesh, in_specs=in_specs, out_specs=out_specs, check_vma=False
    )
```

profile of v0, /device:TPU:0, one launch (start us, length us, event | category | flops | bytes accessed | tf_op | source)
XLA Modules:
  0.0 1129.0 jit_solution(2055085821760850830)
XLA Ops:
  7.2 0.0 all-reduce.10.cloned.1.call-start
  7.2 11.9 %fusion.23 = f32[4096,128]{1,0:T(8,128)} fusion(bf16[2048,4096]{1,0:T(8,128)(2,1)} %param.3, f32[2048,128]{1,0:T(8,128)} %param.4), kind=kOutput, calls=%fused_computation.31 | convolution fusion | flops 2147745792 | bytes 19922944 | tf_op jit(solution)/shard_map/rb,rk->bk/dot_general | solution.py:16
  19.1 0.0 all-reduce.10.cloned.1.call-update
  19.2 0.0 all-reduce.12.cloned.1.call-start
  19.2 128.7 %all-reduce.10.cloned.1.call-done = f32[4096,128]{1,0:T(8,128)} async-done(((f32[4096,128]{1,0:T(8,128)}), f32[4096,128]{1,0:T(8,128)}) %all-reduce.10.cloned.1.call-update) | async-done | bytes 2097168 | tf_op jit(solution)/shard_map/psum | solution.py:18
  147.9 8.1 convolution_bitcast_fusion.4
  156.0 0.0 all-reduce.12.cloned.1.call-update
  156.0 0.0 all-gather.4.cloned.1.call-start
  156.1 125.4 %all-reduce.12.cloned.1.call-done = f32[4096,128]{0,1:T(8,128)} async-done(((f32[4096,128]{0,1:T(8,128)}), f32[4096,128]{0,1:T(8,128)}) %all-reduce.12.cloned.1.call-update) | async-done | bytes 2097168 | tf_op jit(solution)/shard_map/psum | solution.py:23
  281.5 5.6 fusion.9
  287.1 0.0 all-gather.4.cloned.1.call-update
  287.1 0.0 copy-start.4
  287.1 0.2 all-reduce.14.cloned.1.call-start
  287.4 61.0 %all-gather.4.cloned.1.call-done = f32[4096,128]{0,1:T(8,128)} async-done(((f32[256,128]{0,1:T(8,128)}), f32[4096,128]{0,1:T(8,128)}) %all-gather.4.cloned.1.call-update) | async-done | bytes 2097168 | tf_op jit(solution)/shard_map/all_gather | solution.py:25
  348.4 13.0 %convolution_bitcast_fusion.7 = f32[2048,128]{0,1:T(8,128)} fusion(bf16[2048,4096]{1,0:T(8,128)(2,1)} %param.3, f32[4096,128]{0,1:T(8,128)} %all-gather.4.cloned.1.call-done), kind=kOutput, calls=%fused_computation.16 | convolution fusion | flops 2148007936 | bytes 19922944 | tf_op jit(solution)/shard_map/dot_general | solution.py:27
  361.4 0.0 all-reduce.14.cloned.1.call-update
  361.4 0.0 all-reduce.16.cloned.1.call-start
  361.5 0.0 copy-done.4
  361.5 0.3 copy.5
  361.8 17.5 %all-reduce.14.cloned.1.call-done = f32[2048,128]{0,1:T(8,128)} async-done(((f32[2048,128]{0,1:T(8,128)}), f32[2048,128]{0,1:T(8,128)}) %all-reduce.14.cloned.1.call-update) | async-done | bytes 1048592 | tf_op jit(solution)/shard_map/psum | solution.py:28
  379.4 9.8 convolution_bitcast_fusion.1
  389.2 0.0 copy-start
  389.2 0.0 all-reduce.16.cloned.1.call-update
  389.2 0.0 all-reduce.18.cloned.1.call-start
  389.3 1.5 copy-done
  390.8 1.5 broadcast_multiply_fusion
  392.2 124.2 %all-reduce.16.cloned.1.call-done = f32[4096,128]{0,1:T(8,128)} async-done(((f32[4096,128]{0,1:T(8,128)}), f32[4096,128]{0,1:T(8,128)}) %all-reduce.16.cloned.1.call-update) | async-done | bytes 2097168 | tf_op jit(solution)/shard_map/psum | solution.py:18
  516.5 8.0 convolution_bitcast_fusion.3
  524.4 0.0 all-reduce.18.cloned.1.call-update
  524.5 0.3 all-gather.6.cloned.1.call-start
  524.7 125.2 %all-reduce.18.cloned.1.call-done = f32[4096,128]{0,1:T(8,128)} async-done(((f32[4096,128]{0,1:T(8,128)}), f32[4096,128]{0,1:T(8,128)}) %all-reduce.18.cloned.1.call-update) | async-done | bytes 2097168 | tf_op jit(solution)/shard_map/psum | solution.py:23
  649.9 5.6 fusion.12
  655.5 0.0 all-gather.6.cloned.1.call-update
  655.5 0.0 all-reduce.20.cloned.1.call-start
  655.6 61.2 %all-gather.6.cloned.1.call-done = f32[4096,128]{0,1:T(8,128)} async-done(((f32[256,128]{0,1:T(8,128)}), f32[4096,128]{0,1:T(8,128)}) %all-gather.6.cloned.1.call-update) | async-done | bytes 2097168 | tf_op jit(solution)/shard_map/all_gather | solution.py:25
  716.8 13.0 %convolution_bitcast_fusion.6 = f32[2048,128]{0,1:T(8,128)} fusion(bf16[2048,4096]{1,0:T(8,128)(2,1)} %param.3, f32[4096,128]{0,1:T(8,128)} %all-gather.6.cloned.1.call-done), kind=kOutput, calls=%fused_computation.15 | convolution fusion | flops 2148007936 | bytes 19922944 | tf_op jit(solution)/shard_map/dot_general | solution.py:27
  729.8 0.0 all-reduce.20.cloned.1.call-update
  729.8 0.0 all-reduce.22.cloned.1.call-start
  729.9 17.9 %all-reduce.20.cloned.1.call-done = f32[2048,128]{0,1:T(8,128)} async-done(((f32[2048,128]{0,1:T(8,128)}), f32[2048,128]{0,1:T(8,128)}) %all-reduce.20.cloned.1.call-update) | async-done | bytes 1048592 | tf_op jit(solution)/shard_map/psum | solution.py:28
  747.8 10.2 convolution_bitcast_fusion
  758.0 0.0 all-reduce.22.cloned.1.call-update
  758.0 0.3 all-reduce.24.cloned.1.call-start
  758.3 3.2 multiply_add_fusion.1
  761.4 123.8 %all-reduce.22.cloned.1.call-done = f32[4096,128]{0,1:T(8,128)} async-done(((f32[4096,128]{0,1:T(8,128)}), f32[4096,128]{0,1:T(8,128)}) %all-reduce.22.cloned.1.call-update) | async-done | bytes 2097168 | tf_op jit(solution)/shard_map/psum | solution.py:18
  885.2 7.9 convolution_bitcast_fusion.2
  893.2 0.0 all-reduce.24.cloned.1.call-update
  893.2 0.0 all-gather.8.cloned.1.call-start
  893.3 125.4 %all-reduce.24.cloned.1.call-done = f32[4096,128]{0,1:T(8,128)} async-done(((f32[4096,128]{0,1:T(8,128)}), f32[4096,128]{0,1:T(8,128)}) %all-reduce.24.cloned.1.call-update) | async-done | bytes 2097168 | tf_op jit(solution)/shard_map/psum | solution.py:23
  1018.7 5.6 fusion.15
  1024.3 0.0 all-gather.8.cloned.1.call-update
  1024.3 0.0 all-reduce.26.cloned.1.call-start
  1024.4 61.2 %all-gather.8.cloned.1.call-done = f32[4096,128]{0,1:T(8,128)} async-done(((f32[256,128]{0,1:T(8,128)}), f32[4096,128]{0,1:T(8,128)}) %all-gather.8.cloned.1.call-update) | async-done | bytes 2097168 | tf_op jit(solution)/shard_map/all_gather | solution.py:25
  1085.6 0.0 copy-start.2
  1085.6 13.2 %convolution_bitcast_fusion.5 = f32[2048,128]{0,1:T(8,128)} fusion(bf16[2048,4096]{1,0:T(8,128)(2,1)} %param.3, f32[4096,128]{0,1:T(8,128)} %all-gather.8.cloned.1.call-done), kind=kOutput, calls=%fused_computation.14 | convolution fusion | flops 2148007936 | bytes 19922944 | tf_op jit(solution)/shard_map/dot_general | solution.py:27
  1098.7 0.0 all-reduce.26.cloned.1.call-update
  1098.8 0.0 copy-done.2
  1098.8 3.1 multiply_add_fusion
  1101.9 0.0 copy-start.1
  1101.9 3.3 copy.6
  1105.2 11.5 %all-reduce.26.cloned.1.call-done = f32[2048,128]{0,1:T(8,128)} async-done(((f32[2048,128]{0,1:T(8,128)}), f32[2048,128]{0,1:T(8,128)}) %all-reduce.26.cloned.1.call-update) | async-done | bytes 1048592 | tf_op jit(solution)/shard_map/psum | solution.py:28
  1116.7 0.0 copy-done.1
  1116.7 0.0 copy-done.3
  1116.7 2.5 multiply_subtract_fusion
  1119.2 2.5 copy.7
  (1 shorter events, 0.0 us)
Async XLA Ops:
  7.2 140.8 %all-reduce.10.cloned.1.call-start = ((), (), s32[]{:S(2)}) async-start(), calls=%async_computation | async-start | bytes 4194304 | tf_op jit(solution)/shard_map/psum | solution.py:18
  19.2 262.4 %all-reduce.12.cloned.1.call-start = ((), (), s32[]{:S(2)}) async-start(), calls=%async_computation.1 | async-start | bytes 4194304 | tf_op jit(solution)/shard_map/psum | solution.py:23
  156.0 192.4 %all-gather.4.cloned.1.call-start = ((), (), s32[]{:S(2)}) async-start(), calls=%async_computation.2 | async-start | bytes 2228224 | tf_op jit(solution)/shard_map/all_gather | solution.py:25
  287.1 74.4 %copy-start.4 = (f32[2048,128]{1,0:T(8,128)S(1)}, f32[2048,128]{1,0:T(8,128)}, u32[]{:S(2)}) copy-start(f32[2048,128]{1,0:T(8,128)} %param.4) | copy-start | bytes 3145732
  287.1 92.2 %all-reduce.14.cloned.1.call-start = ((), (), s32[]{:S(2)}) async-start(), calls=%async_computation.3 | async-start | bytes 2097152 | tf_op jit(solution)/shard_map/psum | solution.py:28
  361.4 155.1 %all-reduce.16.cloned.1.call-start = ((), (), s32[]{:S(2)}) async-start(), calls=%async_computation.4 | async-start | bytes 4194304 | tf_op jit(solution)/shard_map/psum | solution.py:18
  389.2 1.6 copy-start
  389.2 260.7 %all-reduce.18.cloned.1.call-start = ((), (), s32[]{:S(2)}) async-start(), calls=%async_computation.5 | async-start | bytes 4194304 | tf_op jit(solution)/shard_map/psum | solution.py:23
  524.5 192.3 %all-gather.6.cloned.1.call-start = ((), (), s32[]{:S(2)}) async-start(), calls=%async_computation.6 | async-start | bytes 2228224 | tf_op jit(solution)/shard_map/all_gather | solution.py:25
  655.5 92.3 %all-reduce.20.cloned.1.call-start = ((), (), s32[]{:S(2)}) async-start(), calls=%async_computation.7 | async-start | bytes 2097152 | tf_op jit(solution)/shard_map/psum | solution.py:28
  729.8 155.4 %all-reduce.22.cloned.1.call-start = ((), (), s32[]{:S(2)}) async-start(), calls=%async_computation.8 | async-start | bytes 4194304 | tf_op jit(solution)/shard_map/psum | solution.py:18
  758.0 260.7 %all-reduce.24.cloned.1.call-start = ((), (), s32[]{:S(2)}) async-start(), calls=%async_computation.9 | async-start | bytes 4194304 | tf_op jit(solution)/shard_map/psum | solution.py:23
  893.2 192.3 %all-gather.8.cloned.1.call-start = ((), (), s32[]{:S(2)}) async-start(), calls=%async_computation.10 | async-start | bytes 2228224 | tf_op jit(solution)/shard_map/all_gather | solution.py:25
  1024.3 92.4 %all-reduce.26.cloned.1.call-start = ((), (), s32[]{:S(2)}) async-start(), calls=%async_computation.11 | async-start | bytes 2097152 | tf_op jit(solution)/shard_map/psum | solution.py:28
  1085.6 13.2 %copy-start.2 = (f32[4096,128]{0,1:T(8,128)S(1)}, f32[4096,128]{0,1:T(8,128)}, u32[]{:S(2)}) copy-start(f32[4096,128]{0,1:T(8,128)} %multiply_add_fusion.1) | copy-start | bytes 6291460
  1101.9 14.8 %copy-start.1 = (f32[2048,128]{0,1:T(8,128)S(1)}, f32[2048,128]{0,1:T(8,128)}, u32[]{:S(2)}) copy-start(f32[2048,128]{0,1:T(8,128)} %all-reduce.14.cloned.1.call-done) | copy-start | bytes 3145732
  1101.9 14.8 %copy-start.3 = (f32[2048,128]{0,1:T(8,128)S(1)}, f32[2048,128]{0,1:T(8,128)}, u32[]{:S(2)}) copy-start(f32[2048,128]{0,1:T(8,128)} %all-reduce.20.cloned.1.call-done) | copy-start | bytes 3145732
Sparse Core Ops, SparseCore 0:
  19.3 128.6 all-reduce.9
  156.1 125.3 all-reduce.11
  287.2 61.0 all-gather.3
  361.6 17.7 all-reduce.13
  389.3 127.1 all-reduce.15
  524.6 125.2 all-reduce.17
  655.6 61.0 all-gather.5
  729.9 17.7 all-reduce.19
  758.1 127.1 all-reduce.21
  893.3 125.3 all-reduce.23
  1024.4 61.0 all-gather.7
  1098.9 17.7 all-reduce.25
where the time goes:
time: 1140 us; the launch traced here: 1130 us
  waiting for transfers between devices  983 us (86%)
  matrix products  112 us (10%)
  between operations  14.7 us (1%)
    psum x3, waiting for transfers between devices, run_group(): grad_total = lax.psum(part_grad, 'row')  377 us
    psum x3, waiting for transfers between devices, run_group(): image = lax.psum(term, 'row')  376 us
    all_gather x3, waiting for transfers between devices, run_group(): update = lax.all_gather(update_own, 'row', axis=0, tiled=True)  183 us
    psum x3, waiting for transfers between devices, run_group(): residual = residual - relaxation * lax.psum(change, 'col')  46.9 us
    dot_general x3, matrix products, run_group(): jnp.dot(samples, update.astype(jnp.bfloat16), preferred_element_type=jnp....  39.2 us
    dot_general x3, matrix products, run_group(): jnp.einsum('rb,rk->bk', samples, res16, preferred_element_type=jnp.float32)  31.9 us
    dot_general x3, matrix products, run_group(): term = jnp.dot(inverse, grad_own, precision=lax.Precision.HIGHEST)  24 us
  transfers between devices with their start and end apart: 12, of which 12 were waited for; matrix products, arithmetic and copies ran while one was open for 1% of the time, Pallas kernels for 0%

commit v1 on v0

--- a/solution.py
+++ b/solution.py
@@ -15,9 +15,9 @@
         res16 = residual.astype(jnp.bfloat16)
         part_grad = jnp.einsum("rb,rk->bk", samples, res16, preferred_element_type=jnp.float32)
         own_solution = lax.dynamic_slice_in_dim(solution, offset, own_rows, 0)
-        grad_total = lax.psum(part_grad, "row")
         grad_own = (
-            lax.dynamic_slice_in_dim(grad_total, offset, own_rows, 0) - ridge_weight * own_solution
+            lax.psum_scatter(part_grad, "row", scatter_dimension=0, tiled=True)
+            - ridge_weight * own_solution
         )
         term = jnp.dot(inverse, grad_own, precision=lax.Precision.HIGHEST)
         image = lax.psum(term, "row")

time: 1140 us -> 994 us (0.87)
  waiting for transfers between devices: 983 us -> 841 us
    psum x3 -> x0, waiting for transfers between devices: 377 us -> none  [run_group(): grad_total = lax.psum(part_grad, 'row')]
    reduce_scatter x0 -> x3, waiting for transfers between devices: none -> 241 us  [run_group(): lax.psum_scatter(part_grad, 'row', scatter_dimension=0, tiled=True)]
where the time goes in v1:
time: 994 us; the launch traced here: 986 us
  waiting for transfers between devices  841 us (85%)
  matrix products  112 us (11%)
  between operations  14.7 us (1%)
  other arithmetic  10.3 us (1%)
    psum x3, waiting for transfers between devices, run_group(): image = lax.psum(term, 'row')  369 us
    reduce_scatter x3, waiting for transfers between devices, run_group(): lax.psum_scatter(part_grad, 'row', scatter_dimension=0, tiled=True)  241 us
    all_gather x3, waiting for transfers between devices, run_group(): update = lax.all_gather(update_own, 'row', axis=0, tiled=True)  183 us
    psum x3, waiting for transfers between devices, run_group(): residual = residual - relaxation * lax.psum(change, 'col')  46.9 us
    dot_general x3, matrix products, run_group(): jnp.dot(samples, update.astype(jnp.bfloat16), preferred_element_type=jnp....  39.2 us
    dot_general x3, matrix products, run_group(): jnp.einsum('rb,rk->bk', samples, res16, preferred_element_type=jnp.float32)  31.9 us
    dot_general x3, matrix products, run_group(): term = jnp.dot(inverse, grad_own, precision=lax.Precision.HIGHEST)  23.9 us
  transfers between devices with their start and end apart: 12, of which 12 were waited for; matrix products, arithmetic and copies ran while one was open for 1% of the time, Pallas kernels for 0%

profile of v1, /device:TPU:0, one launch (start us, length us, event | category | flops | bytes accessed | tf_op | source)
XLA Modules:
  0.0 986.2 jit_solution(3133331421541427131)
XLA Ops:
  7.2 0.0 reduce-scatter.4.cloned.1.call-start
  7.2 11.9 %fusion.23 = f32[4096,128]{1,0:T(8,128)} fusion(bf16[2048,4096]{1,0:T(8,128)(2,1)} %param.3, f32[2048,128]{1,0:T(8,128)} %param.4), kind=kOutput, calls=%fused_computation.31 | convolution fusion | flops 2147745792 | bytes 19922944 | tf_op jit(solution)/shard_map/rb,rk->bk/dot_general | solution.py:16
  19.1 0.0 reduce-scatter.4.cloned.1.call-update
  19.2 0.0 all-reduce.7.cloned.1.call-start
  19.2 83.6 %reduce-scatter.4.cloned.1.call-done = f32[256,128]{1,0:T(8,128)} async-done(((f32[4096,128]{1,0:T(8,128)}), f32[256,128]{1,0:T(8,128)}) %reduce-scatter.4.cloned.1.call-update) | async-done | bytes 131088 | tf_op jit(solution)/shard_map/reduce_scatter | solution.py:19
  102.8 8.1 convolution_bitcast_fusion.4
  110.8 0.0 all-reduce.7.cloned.1.call-update
  110.8 0.0 all-gather.4.cloned.1.call-start
  110.9 123.2 %all-reduce.7.cloned.1.call-done = f32[4096,128]{0,1:T(8,128)} async-done(((f32[4096,128]{0,1:T(8,128)}), f32[4096,128]{0,1:T(8,128)}) %all-reduce.7.cloned.1.call-update) | async-done | bytes 2097168 | tf_op jit(solution)/shard_map/psum | solution.py:23
  234.1 5.6 fusion.9
  239.7 0.0 all-gather.4.cloned.1.call-update
  239.7 0.0 copy-start.4
  239.7 0.2 all-reduce.9.cloned.1.call-start
  239.9 61.0 %all-gather.4.cloned.1.call-done = f32[4096,128]{0,1:T(8,128)} async-done(((f32[256,128]{0,1:T(8,128)}), f32[4096,128]{0,1:T(8,128)}) %all-gather.4.cloned.1.call-update) | async-done | bytes 2097168 | tf_op jit(solution)/shard_map/all_gather | solution.py:25
  301.0 13.0 %convolution_bitcast_fusion.7 = f32[2048,128]{0,1:T(8,128)} fusion(bf16[2048,4096]{1,0:T(8,128)(2,1)} %param.3, f32[4096,128]{0,1:T(8,128)} %all-gather.4.cloned.1.call-done), kind=kOutput, calls=%fused_computation.16 | convolution fusion | flops 2148007936 | bytes 19922944 | tf_op jit(solution)/shard_map/dot_general | solution.py:27
  314.0 0.0 all-reduce.9.cloned.1.call-update
  314.0 0.0 reduce-scatter.6.cloned.1.call-start
  314.1 0.0 copy-done.4
  314.1 0.3 copy.5
  314.4 17.5 %all-reduce.9.cloned.1.call-done = f32[2048,128]{0,1:T(8,128)} async-done(((f32[2048,128]{0,1:T(8,128)}), f32[2048,128]{0,1:T(8,128)}) %all-reduce.9.cloned.1.call-update) | async-done | bytes 1048592 | tf_op jit(solution)/shard_map/psum | solution.py:28
  332.0 9.8 convolution_bitcast_fusion.1
  341.7 0.0 copy-start
  341.7 0.0 reduce-scatter.6.cloned.1.call-update
  341.8 0.0 all-reduce.11.cloned.1.call-start
  341.8 1.5 copy-done
  343.3 1.5 broadcast_multiply_fusion
  344.8 78.9 %reduce-scatter.6.cloned.1.call-done = f32[256,128]{0,1:T(8,128)} async-done(((f32[4096,128]{0,1:T(8,128)}), f32[256,128]{0,1:T(8,128)}) %reduce-scatter.6.cloned.1.call-update) | async-done | bytes 131088 | tf_op jit(solution)/shard_map/reduce_scatter | solution.py:19
  423.7 7.9 convolution_bitcast_fusion.3
  431.7 0.0 all-reduce.11.cloned.1.call-update
  431.7 0.3 all-gather.6.cloned.1.call-start
  431.9 123.0 %all-reduce.11.cloned.1.call-done = f32[4096,128]{0,1:T(8,128)} async-done(((f32[4096,128]{0,1:T(8,128)}), f32[4096,128]{0,1:T(8,128)}) %all-reduce.11.cloned.1.call-update) | async-done | bytes 2097168 | tf_op jit(solution)/shard_map/psum | solution.py:23
  555.0 5.6 fusion.12
  560.5 0.0 all-gather.6.cloned.1.call-update
  560.6 0.0 all-reduce.13.cloned.1.call-start
  560.6 61.2 %all-gather.6.cloned.1.call-done = f32[4096,128]{0,1:T(8,128)} async-done(((f32[256,128]{0,1:T(8,128)}), f32[4096,128]{0,1:T(8,128)}) %all-gather.6.cloned.1.call-update) | async-done | bytes 2097168 | tf_op jit(solution)/shard_map/all_gather | solution.py:25
  621.8 13.0 %convolution_bitcast_fusion.6 = f32[2048,128]{0,1:T(8,128)} fusion(bf16[2048,4096]{1,0:T(8,128)(2,1)} %param.3, f32[4096,128]{0,1:T(8,128)} %all-gather.6.cloned.1.call-done), kind=kOutput, calls=%fused_computation.15 | convolution fusion | flops 2148007936 | bytes 19922944 | tf_op jit(solution)/shard_map/dot_general | solution.py:27
  634.9 0.0 all-reduce.13.cloned.1.call-update
  634.9 0.0 reduce-scatter.8.cloned.1.call-start
  634.9 17.9 %all-reduce.13.cloned.1.call-done = f32[2048,128]{0,1:T(8,128)} async-done(((f32[2048,128]{0,1:T(8,128)}), f32[2048,128]{0,1:T(8,128)}) %all-reduce.13.cloned.1.call-update) | async-done | bytes 1048592 | tf_op jit(solution)/shard_map/psum | solution.py:28
  652.8 10.2 %convolution_bitcast_fusion = f32[4096,128]{0,1:T(8,128)} fusion(bf16[2048,4096]{1,0:T(8,128)(2,1)} %param.3, f32[2048,128]{0,1:T(8,128)} %all-reduce.13.cloned.1.call-done, f32[2048,128]{0,1:T(8,128)S(1)} %copy.5, f32[2048,128]{0,1:T(8,128)} %all-reduce.9.cloned.1.call-done), kind=kOutput, calls=%fused_computation | convolution fusion | flops 2148794368 | bytes 22020096 | tf_op jit(solution)/shard_map/rb,rk->bk/dot_general | solution.py:16
  663.0 0.0 reduce-scatter.8.cloned.1.call-update
  663.0 0.3 all-reduce.15.cloned.1.call-start
  663.3 3.2 multiply_add_fusion.1
  666.5 78.6 %reduce-scatter.8.cloned.1.call-done = f32[256,128]{0,1:T(8,128)} async-done(((f32[4096,128]{0,1:T(8,128)}), f32[256,128]{0,1:T(8,128)}) %reduce-scatter.8.cloned.1.call-update) | async-done | bytes 131088 | tf_op jit(solution)/shard_map/reduce_scatter | solution.py:19
  745.0 7.9 convolution_bitcast_fusion.2
  753.0 0.0 all-reduce.15.cloned.1.call-update
  753.0 0.0 all-gather.8.cloned.1.call-start
  753.1 122.8 %all-reduce.15.cloned.1.call-done = f32[4096,128]{0,1:T(8,128)} async-done(((f32[4096,128]{0,1:T(8,128)}), f32[4096,128]{0,1:T(8,128)}) %all-reduce.15.cloned.1.call-update) | async-done | bytes 2097168 | tf_op jit(solution)/shard_map/psum | solution.py:23
  875.9 5.6 fusion.15
  881.5 0.0 all-gather.8.cloned.1.call-update
  881.5 0.0 all-reduce.17.cloned.1.call-start
  881.5 61.2 %all-gather.8.cloned.1.call-done = f32[4096,128]{0,1:T(8,128)} async-done(((f32[256,128]{0,1:T(8,128)}), f32[4096,128]{0,1:T(8,128)}) %all-gather.8.cloned.1.call-update) | async-done | bytes 2097168 | tf_op jit(solution)/shard_map/all_gather | solution.py:25
  942.8 0.0 copy-start.2
  942.8 13.2 %convolution_bitcast_fusion.5 = f32[2048,128]{0,1:T(8,128)} fusion(bf16[2048,4096]{1,0:T(8,128)(2,1)} %param.3, f32[4096,128]{0,1:T(8,128)} %all-gather.8.cloned.1.call-done), kind=kOutput, calls=%fused_computation.14 | convolution fusion | flops 2148007936 | bytes 19922944 | tf_op jit(solution)/shard_map/dot_general | solution.py:27
  955.9 0.0 all-reduce.17.cloned.1.call-update
  955.9 0.0 copy-done.2
  956.0 3.1 multiply_add_fusion
  959.1 0.0 copy-start.1
  959.1 3.3 copy.6
  962.4 11.5 %all-reduce.17.cloned.1.call-done = f32[2048,128]{0,1:T(8,128)} async-done(((f32[2048,128]{0,1:T(8,128)}), f32[2048,128]{0,1:T(8,128)}) %all-reduce.17.cloned.1.call-update) | async-done | bytes 1048592 | tf_op jit(solution)/shard_map/psum | solution.py:28
  973.9 0.0 copy-done.1
  973.9 0.0 copy-done.3
  973.9 2.5 multiply_subtract_fusion
  976.4 2.5 copy.7
  (1 shorter events, 0.0 us)
Async XLA Ops:
  7.2 95.6 %reduce-scatter.4.cloned.1.call-start = ((), (), s32[]{:S(2)}) async-start(), calls=%async_computation.3 | async-start | bytes 2228224 | tf_op jit(solution)/shard_map/reduce_scatter | solution.py:19
  19.2 215.0 %all-reduce.7.cloned.1.call-start = ((), (), s32[]{:S(2)}) async-start(), calls=%async_computation.4 | async-start | bytes 4194304 | tf_op jit(solution)/shard_map/psum | solution.py:23
  110.8 190.1 %all-gather.4.cloned.1.call-start = ((), (), s32[]{:S(2)}) async-start(), calls=%async_computation.5 | async-start | bytes 2228224 | tf_op jit(solution)/shard_map/all_gather | solution.py:25
  239.7 74.4 %copy-start.4 = (f32[2048,128]{1,0:T(8,128)S(1)}, f32[2048,128]{1,0:T(8,128)}, u32[]{:S(2)}) copy-start(f32[2048,128]{1,0:T(8,128)} %param.4) | copy-start | bytes 3145732
  239.7 92.2 %all-reduce.9.cloned.1.call-start = ((), (), s32[]{:S(2)}) async-start(), calls=%async_computation.6 | async-start | bytes 2097152 | tf_op jit(solution)/shard_map/psum | solution.py:28
  314.0 109.7 %reduce-scatter.6.cloned.1.call-start = ((), (), s32[]{:S(2)}) async-start(), calls=%async_computation.7 | async-start | bytes 2228224 | tf_op jit(solution)/shard_map/reduce_scatter | solution.py:19
  341.7 1.6 copy-start
  341.8 213.2 %all-reduce.11.cloned.1.call-start = ((), (), s32[]{:S(2)}) async-start(), calls=%async_computation.8 | async-start | bytes 4194304 | tf_op jit(solution)/shard_map/psum | solution.py:23
  431.7 190.2 %all-gather.6.cloned.1.call-start = ((), (), s32[]{:S(2)}) async-start(), calls=%async_computation.9 | async-start | bytes 2228224 | tf_op jit(solution)/shard_map/all_gather | solution.py:25
  560.6 92.3 %all-reduce.13.cloned.1.call-start = ((), (), s32[]{:S(2)}) async-start(), calls=%async_computation.10 | async-start | bytes 2097152 | tf_op jit(solution)/shard_map/psum | solution.py:28
  634.9 110.2 %reduce-scatter.8.cloned.1.call-start = ((), (), s32[]{:S(2)}) async-start(), calls=%async_computation.11 | async-start | bytes 2228224 | tf_op jit(solution)/shard_map/reduce_scatter | solution.py:19
  663.0 212.9 %all-reduce.15.cloned.1.call-start = ((), (), s32[]{:S(2)}) async-start(), calls=%async_computation.12 | async-start | bytes 4194304 | tf_op jit(solution)/shard_map/psum | solution.py:23
  753.0 189.7 %all-gather.8.cloned.1.call-start = ((), (), s32[]{:S(2)}) async-start(), calls=%async_computation.13 | async-start | bytes 2228224 | tf_op jit(solution)/shard_map/all_gather | solution.py:25
  881.5 92.4 %all-reduce.17.cloned.1.call-start = ((), (), s32[]{:S(2)}) async-start(), calls=%async_computation.14 | async-start | bytes 2097152 | tf_op jit(solution)/shard_map/psum | solution.py:28
  942.8 13.2 %copy-start.2 = (f32[4096,128]{0,1:T(8,128)S(1)}, f32[4096,128]{0,1:T(8,128)}, u32[]{:S(2)}) copy-start(f32[4096,128]{0,1:T(8,128)} %multiply_add_fusion.1) | copy-start | bytes 6291460
  959.1 14.8 %copy-start.1 = (f32[2048,128]{0,1:T(8,128)S(1)}, f32[2048,128]{0,1:T(8,128)}, u32[]{:S(2)}) copy-start(f32[2048,128]{0,1:T(8,128)} %all-reduce.9.cloned.1.call-done) | copy-start | bytes 3145732
  959.1 14.8 %copy-start.3 = (f32[2048,128]{0,1:T(8,128)S(1)}, f32[2048,128]{0,1:T(8,128)}, u32[]{:S(2)}) copy-start(f32[2048,128]{0,1:T(8,128)} %all-reduce.13.cloned.1.call-done) | copy-start | bytes 3145732
Sparse Core Ops, SparseCore 0:
  19.3 83.4 reduce-scatter.3
  111.0 123.0 all-reduce.6
  239.8 61.0 all-gather.3
  314.1 17.7 all-reduce.8
  341.9 81.7 reduce-scatter.5
  431.8 123.1 all-reduce.10
  560.7 61.0 all-gather.5
  635.0 17.7 all-reduce.12
  663.2 81.8 reduce-scatter.7
  753.1 122.7 all-reduce.14
  881.6 61.0 all-gather.7
  956.1 17.7 all-reduce.16

commit v2 on v1

--- a/solution.py
+++ b/solution.py
@@ -1,12 +1,141 @@
+import functools
+
 import jax
 import jax.numpy as jnp
 from jax import lax
+from jax.experimental import pallas as pl
+from jax.experimental.pallas import tpu as pltpu
 from jax.sharding import PartitionSpec as P
 
 ROUNDS = 3
+PARTS = 4
 
 
 ridge_weight = 0.5
+
+
+def bit_orders(nbits):
+    if nbits == 4:
+        return [(3, 2, 1, 0), (2, 3, 0, 1), (1, 3, 2, 0), (0, 2, 3, 1)]
+    return [tuple((nbits - 1 - p - t) % nbits for t in range(nbits)) for p in range(PARTS)]
+
+
+def exchange_kernel(axis, nbits, reduce, gather, x_ref, out_ref, send_sem, recv_sem, *scratch):
+    me = lax.axis_index(axis)
+    bits = [lax.rem(lax.div(me, 2**b), 2) for b in range(nbits)]
+    partner = [me + (1 - 2 * bits[b]) * 2**b for b in range(nbits)]
+    orders = bit_orders(nbits)
+    rows = (x_ref if not reduce else out_ref if not gather else x_ref).shape[-2] // PARTS
+    span = [pl.ds(p * rows, rows) for p in range(PARTS)]
+
+    def index(p, free, flip=None):
+        lead = []
+        for b in reversed(range(nbits)):
+            if b in free:
+                lead.append(slice(None))
+            else:
+                lead.append(1 - bits[b] if b == flip else bits[b])
+        return tuple(lead) + (span[p], slice(None))
+
+    def own(p):
+        return index(p, ()) if gather else (span[p], slice(None))
+
+    barrier = pltpu.get_barrier_semaphore()
+    for b in range(nbits):
+        pl.semaphore_signal(
+            barrier, inc=1, device_id={axis: partner[b]}, device_id_type=pl.DeviceIdType.MESH
+        )
+    pl.semaphore_wait(barrier, nbits)
+
+    def start(p, step, source, target, b):
+        copy = pltpu.make_async_remote_copy(
+            src_ref=source,
+            dst_ref=target,
+            send_sem=send_sem.at[p, step],
+            recv_sem=recv_sem.at[p, step],
+            device_id={axis: partner[b]},
+            device_id_type=pl.DeviceIdType.MESH,
+        )
+        copy.start()
+        return copy
+
+    live = [None] * PARTS
+    step = 0
+    if reduce:
+        acc, arrived = scratch[0], scratch[1:]
+
+        def landing(p, t):
+            return (slice(None),) * (nbits - 1 - t) + (span[p], slice(None))
+
+        def add(p, t):
+            live[p].wait()
+            keep = index(p, orders[p][: nbits - 1 - t])
+            source = x_ref if t == 0 else acc
+            value = source[keep] + arrived[t][landing(p, t)]
+            if t == nbits - 1:
+                out_ref[own(p)] = value
+            else:
+                acc[keep] = value
+
+        for t in range(nbits):
+            for p in range(PARTS):
+                if t > 0:
+                    add(p, t - 1)
+                b = orders[p][nbits - 1 - t]
+                source = x_ref if t == 0 else acc
+                live[p] = start(
+                    p,
+                    step,
+                    source.at[index(p, orders[p][: nbits - 1 - t], b)],
+                    arrived[t].at[landing(p, t)],
+                    b,
+                )
+            step += 1
+    for t in range(nbits if gather else 0):
+        for p in range(PARTS):
+            if t > 0:
+                live[p].wait()
+            elif reduce:
+                add(p, nbits - 1)
+            else:
+                out_ref[own(p)] = x_ref[span[p], :]
+            piece = out_ref.at[index(p, orders[p][:t])]
+            live[p] = start(p, step, piece, piece, orders[p][t])
+        step += 1
+    for p in range(PARTS):
+        if gather:
+            live[p].wait()
+        else:
+            add(p, nbits - 1)
+
+
+def exchange(x, axis, collective_id, reduce, gather):
+    n = lax.axis_size(axis)
+    nbits = n.bit_length() - 1
+    width = x.shape[1]
+    block = x.shape[0] // n if reduce else x.shape[0]
+    whole = (2,) * nbits + (block, width)
+    scratch = []
+    if reduce:
+        scratch.append(pltpu.VMEM(whole, jnp.float32))
+        for t in range(nbits):
+            scratch.append(pltpu.VMEM((2,) * (nbits - 1 - t) + (block, width), jnp.float32))
+    steps = nbits * (int(reduce) + int(gather))
+    out = pl.pallas_call(
+        functools.partial(exchange_kernel, axis, nbits, reduce, gather),
+        out_shape=jax.ShapeDtypeStruct(whole if gather else (block, width), jnp.float32),
+        in_specs=[pl.BlockSpec(memory_space=pltpu.VMEM)],
+        out_specs=pl.BlockSpec(memory_space=pltpu.VMEM),
+        scratch_shapes=[
+            pltpu.SemaphoreType.DMA((PARTS, steps)),
+            pltpu.SemaphoreType.DMA((PARTS, steps)),
+        ]
+        + scratch,
+        compiler_params=pltpu.CompilerParams(
+            collective_id=collective_id, has_side_effects=True, vmem_limit_bytes=24 << 20
+        ),
+    )(x.reshape(whole) if reduce else x)
+    return out.reshape(-1, width)
 
 
 def run_group(samples, residual, inverse, own_rows, offset, relaxation):
@@ -15,17 +144,14 @@
         res16 = residual.astype(jnp.bfloat16)
         part_grad = jnp.einsum("rb,rk->bk", samples, res16, preferred_element_type=jnp.float32)
         own_solution = lax.dynamic_slice_in_dim(solution, offset, own_rows, 0)
-        grad_own = (
-            lax.psum_scatter(part_grad, "row", scatter_dimension=0, tiled=True)
-            - ridge_weight * own_solution
-        )
+        grad_own = exchange(part_grad, "row", 0, True, False) - ridge_weight * own_solution
         term = jnp.dot(inverse, grad_own, precision=lax.Precision.HIGHEST)
-        image = lax.psum(term, "row")
+        image = exchange(term, "row", 1, True, True)
         update_own = jnp.einsum("bc,bk->ck", inverse, image, precision=lax.Precision.HIGHEST)
-        update = lax.all_gather(update_own, "row", axis=0, tiled=True)
+        update = exchange(update_own, "row", 2, False, True)
         solution = solution + relaxation * update
         change = jnp.dot(samples, update.astype(jnp.bfloat16), preferred_element_type=jnp.float32)
-        residual = residual - relaxation * lax.psum(change, "col")
+        residual = residual - relaxation * exchange(change, "col", 3, True, True)
     return (solution, residual)
 
 

time: 994 us -> 454 us (0.46)
  waiting for transfers between devices: 841 us -> 0 us
  Pallas kernels: 0 us -> 320 us
  between operations: 14.7 us -> 1.21 us
    psum x6 -> x0, waiting for transfers between devices: 416 us -> none  [the longest x3 369 us: run_group(): image = lax.psum(term, 'row')]
    pallas_call x0 -> x12, Pallas kernels: none -> 320 us  [exchange(): pl.pallas_call(functools.partial(exchange_kernel, axis, nbits, reduce, ga...]
    reduce_scatter x3 -> x0, waiting for transfers between devices: 241 us -> none  [run_group(): lax.psum_scatter(part_grad, 'row', scatter_dimension=0, tiled=True)]
    all_gather x3 -> x0, waiting for transfers between devices: 183 us -> none  [run_group(): update = lax.all_gather(update_own, 'row', axis=0, tiled=True)]
    dot_general x0 -> x8, local copies, waits for them, and re-layouts: none -> 11.1 us  [the longest x3 6.36 us: run_group(): term = jnp.dot(inverse, grad_own, precision=lax.Precision.HIGHEST)]
  transfers between devices with their start and end apart: 12 -> 0, of which waited for: 12 -> 0; matrix products, arithmetic and copies ran while one was open for 1% -> 0% of each run, Pallas kernels for 0% -> 0%
where the time goes in v2:
time: 454 us; the launch traced here: 449 us
  Pallas kernels  320 us (70%)
  matrix products  104 us (23%)
  local copies, waits for them, and re-layouts  14.9 us (3%)
  other arithmetic  8.49 us (2%)
    pallas_call x12, Pallas kernels, exchange(): pl.pallas_call(functools.partial(exchange_kernel, axis, nbits, reduce, ga...  320 us
    dot_general x3, matrix products, run_group(): jnp.dot(samples, update.astype(jnp.bfloat16), preferred_element_type=jnp....  34.4 us
    dot_general x3, matrix products, run_group(): jnp.einsum('rb,rk->bk', samples, res16, preferred_element_type=jnp.float32)  27.6 us
    dot_general x3, matrix products, run_group(): term = jnp.dot(inverse, grad_own, precision=lax.Precision.HIGHEST)  22 us
    dot_general x3, matrix products, run_group(): jnp.einsum('bc,bk->ck', inverse, image, precision=lax.Precision.HIGHEST)  20 us

profile of v2, /device:TPU:0, one launch (start us, length us, event | category | flops | bytes accessed | tf_op | source)
XLA Modules:
  0.0 448.7 jit_solution(11422795844296807595)
XLA Ops:
  0.6 0.0 copy-start
  0.6 8.7 %fusion.20 = f32[4096,128]{1,0:T(8,128)S(1)} fusion(bf16[2048,4096]{1,0:T(8,128)(2,1)} %param.3, f32[2048,128]{1,0:T(8,128)} %param.4), kind=kOutput, calls=%fused_computation.33 | convolution fusion | flops 2147745792 | bytes 19922944 | tf_op jit(solution)/shard_map/rb,rk->bk/dot_general | solution.py:145
  9.3 35.2 %shard_map.50 = f32[256,128]{1,0:T(8,128)S(1)} custom-call(f32[2,2,2,2,256,128]{5,4,3,2,1,0:T(8,128)S(1)} %bitcast.84), custom_call_target="tpu_custom_call" | custom-call | tf_op jit(solution)/shard_map/pallas_call | solution.py:124
  44.5 0.0 copy-done
  44.5 5.8 %convolution_bitcast_fusion.4 = f32[4096,128]{0,1:T(8,128)} fusion(f32[256,128]{1,0:T(8,128)S(1)} %shard_map.50, f32[1,4096,256]{2,1,0:T(8,128)S(1)} %copy-done), kind=kOutput, calls=%fused_computation.4 | convolution fusion | flops 1610612736 | bytes 6422528 | tf_op jit(solution)/shard_map/dot_general | solution.py:148
  50.3 2.4 copy.5
  52.7 0.0 copy-start.1
  52.7 46.4 %shard_map.51 = f32[2,2,2,2,256,128]{5,4,3,2,1,0:T(8,128)S(1)} custom-call(f32[2,2,2,2,256,128]{5,4,3,2,1,0:T(8,128)S(1)} %bitcast.88), custom_call_target="tpu_custom_call" | custom-call | tf_op jit(solution)/shard_map/pallas_call | solution.py:124
  99.1 0.0 copy-done.1
  99.1 6.7 %fusion.9.x_ref = f32[256,128]{1,0:T(8,128)S(1)} fusion(f32[4096,128]{1,0:T(8,128)S(1)} %bitcast.85, f32[1,4096,256]{2,1,0:T(8,128)S(1)} %copy-done.1), kind=kOutput, calls=%fused_computation.19 | convolution fusion | flops 1610612736 | bytes 6422528 | tf_op jit(solution)/shard_map/bc,bk->ck/dot_general | solution.py:150
  105.8 22.3 %shard_map.52 = f32[2,2,2,2,256,128]{5,4,3,2,1,0:T(8,128)S(1)} custom-call(f32[256,128]{1,0:T(8,128)S(1)} %fusion.9.x_ref), custom_call_target="tpu_custom_call" | custom-call | tf_op jit(solution)/shard_map/pallas_call | solution.py:124
  128.1 1.7 broadcast_multiply_fusion.2
  129.7 11.5 %convolution_bitcast_fusion.7 = f32[2048,128]{0,1:T(8,128)S(1)} fusion(bf16[4096,128]{1,0:T(8,128)(2,1)S(1)} %bitcast.98, bf16[2048,4096]{1,0:T(8,128)(2,1)} %param.3), kind=kOutput, calls=%fused_computation.16 | convolution fusion | flops 2147483648 | bytes 18874368 | tf_op jit(solution)/shard_map/dot_general | solution.py:153
  141.2 0.3 copy.7
  141.5 0.0 copy-start.4
  141.5 3.1 shard_map.53
  144.6 0.1 broadcast_multiply_fusion.5
  144.7 0.0 copy-start.6
  144.7 1.0 copy-done.6
  145.7 0.0 copy-done.4
  145.7 0.3 bitcast_subtract_fusion.2
  146.0 9.5 %convolution_bitcast_fusion.1 = f32[4096,128]{0,1:T(8,128)} fusion(bf16[2048,4096]{1,0:T(8,128)(2,1)} %param.3, bf16[2048,128]{1,0:T(8,128)(2,1)S(1)} %bitcast_subtract_fusion.2), kind=kOutput, calls=%fused_computation.1 | convolution fusion | flops 2147483648 | bytes 19398656 | tf_op jit(solution)/shard_map/rb,rk->bk/dot_general | solution.py:145
  155.5 1.9 copy.8
  157.4 32.5 %shard_map.54 = f32[256,128]{1,0:T(8,128)S(1)} custom-call(f32[2,2,2,2,256,128]{5,4,3,2,1,0:T(8,128)S(1)} %bitcast.89), custom_call_target="tpu_custom_call" | custom-call | tf_op jit(solution)/shard_map/pallas_call | solution.py:124
  189.9 8.1 %convolution_bitcast_fusion.3 = f32[4096,128]{0,1:T(8,128)} fusion(f32[1,4096,256]{2,1,0:T(8,128)} %param.5, f32[256,128]{1,0:T(8,128)S(1)} %shard_map.54, f32[4096,128]{1,0:T(8,128)} %bitcast.96, s32[]{:T(128)S(6)} %select_n.4), kind=kOutput, calls=%fused_computation.3 | convolution fusion | flops 1610678272 | bytes 6553604 | tf_op jit(solution)/shard_map/dot_general | solution.py:148
  198.0 1.9 copy.9
  199.9 0.0 copy-start.2
  199.9 48.5 %shard_map.55 = f32[2,2,2,2,256,128]{5,4,3,2,1,0:T(8,128)S(1)} custom-call(f32[2,2,2,2,256,128]{5,4,3,2,1,0:T(8,128)S(1)} %bitcast.90), custom_call_target="tpu_custom_call" | custom-call | tf_op jit(solution)/shard_map/pallas_call | solution.py:124
  248.4 0.0 copy-done.2
  248.5 6.7 %fusion.12.x_ref = f32[256,128]{1,0:T(8,128)S(1)} fusion(f32[4096,128]{1,0:T(8,128)S(1)} %bitcast.86, f32[1,4096,256]{2,1,0:T(8,128)S(1)} %copy-done.2), kind=kOutput, calls=%fused_computation.20 | convolution fusion | flops 1610612736 | bytes 6422528 | tf_op jit(solution)/shard_map/bc,bk->ck/dot_general | solution.py:150
  255.1 23.4 %shard_map.56 = f32[2,2,2,2,256,128]{5,4,3,2,1,0:T(8,128)S(1)} custom-call(f32[256,128]{1,0:T(8,128)S(1)} %fusion.12.x_ref), custom_call_target="tpu_custom_call" | custom-call | tf_op jit(solution)/shard_map/pallas_call | solution.py:124
  278.5 0.0 copy-start.9
  278.5 0.3 fusion.35
  278.9 1.2 copy-done.9
  280.1 1.5 bitcast_add_fusion.1
  281.6 11.5 %convolution_bitcast_fusion.6 = f32[2048,128]{0,1:T(8,128)S(1)} fusion(bf16[4096,128]{1,0:T(8,128)(2,1)S(1)} %bitcast.97, bf16[2048,4096]{1,0:T(8,128)(2,1)} %param.3), kind=kOutput, calls=%fused_computation.15 | convolution fusion | flops 2147483648 | bytes 18874368 | tf_op jit(solution)/shard_map/dot_general | solution.py:153
  293.1 0.3 copy.11
  293.4 0.0 copy-start.5
  293.4 0.0 copy-start.7
  293.5 3.5 shard_map.57
  296.9 0.1 broadcast_multiply_fusion.4
  297.0 0.0 copy-done.5
  297.0 0.0 copy-done.7
  297.0 0.2 bitcast_subtract_fusion.1
  297.2 9.5 %convolution_bitcast_fusion = f32[4096,128]{0,1:T(8,128)} fusion(bf16[2048,4096]{1,0:T(8,128)(2,1)} %param.3, f32[2048,128]{1,0:T(8,128)S(1)} %bitcast_subtract_fusion.1), kind=kOutput, calls=%fused_computation | convolution fusion | flops 2147745792 | bytes 19922944 | tf_op jit(solution)/shard_map/rb,rk->bk/dot_general | solution.py:145
  306.7 1.9 copy.12
  308.6 31.8 %shard_map.58 = f32[256,128]{1,0:T(8,128)S(1)} custom-call(f32[2,2,2,2,256,128]{5,4,3,2,1,0:T(8,128)S(1)} %bitcast.91), custom_call_target="tpu_custom_call" | custom-call | tf_op jit(solution)/shard_map/pallas_call | solution.py:124
  340.4 8.1 %convolution_bitcast_fusion.2 = f32[4096,128]{0,1:T(8,128)} fusion(f32[1,4096,256]{2,1,0:T(8,128)} %param.5, f32[256,128]{1,0:T(8,128)S(1)} %shard_map.58, f32[4096,128]{1,0:T(8,128)} %bitcast_add_fusion.1, s32[]{:T(128)S(6)} %select_n.4), kind=kOutput, calls=%fused_computation.2 | convolution fusion | flops 1610678272 | bytes 6553604 | tf_op jit(solution)/shard_map/dot_general | solution.py:148
  348.5 2.1 copy.13
  350.6 0.0 copy-start.3
  350.6 47.8 %shard_map.59 = f32[2,2,2,2,256,128]{5,4,3,2,1,0:T(8,128)S(1)} custom-call(f32[2,2,2,2,256,128]{5,4,3,2,1,0:T(8,128)S(1)} %bitcast.92), custom_call_target="tpu_custom_call" | custom-call | tf_op jit(solution)/shard_map/pallas_call | solution.py:124
  398.4 0.0 copy-done.3
  398.4 6.7 %fusion.15.x_ref = f32[256,128]{1,0:T(8,128)S(1)} fusion(f32[4096,128]{1,0:T(8,128)S(1)} %bitcast.87, f32[1,4096,256]{2,1,0:T(8,128)S(1)} %copy-done.3), kind=kOutput, calls=%fused_computation.21 | convolution fusion | flops 1610612736 | bytes 6422528 | tf_op jit(solution)/shard_map/bc,bk->ck/dot_general | solution.py:150
  405.1 22.7 %shard_map.60 = f32[2,2,2,2,256,128]{5,4,3,2,1,0:T(8,128)S(1)} custom-call(f32[256,128]{1,0:T(8,128)S(1)} %fusion.15.x_ref), custom_call_target="tpu_custom_call" | custom-call | tf_op jit(solution)/shard_map/pallas_call | solution.py:124
  427.8 1.7 fusion.34
  429.4 11.5 %convolution_bitcast_fusion.5 = f32[2048,128]{0,1:T(8,128)S(1)} fusion(bf16[4096,128]{1,0:T(8,128)(2,1)S(1)} %bitcast.99, bf16[2048,4096]{1,0:T(8,128)(2,1)} %param.3), kind=kOutput, calls=%fused_computation.14 | convolution fusion | flops 2147483648 | bytes 18874368 | tf_op jit(solution)/shard_map/dot_general | solution.py:153
  440.9 0.3 copy.15
  441.2 3.1 shard_map.61
  444.3 0.1 broadcast_multiply_fusion.3
  444.4 0.0 copy-start.8
  444.4 1.1 bitcast_subtract_fusion
  445.5 0.8 copy-done.10
  446.3 0.7 copy-done.8
  446.9 1.5 bitcast_add_fusion
  (1 shorter events, 0.0 us)
Async XLA Ops:
  0.6 43.9 %copy-start = (f32[1,4096,256]{2,1,0:T(8,128)S(1)}, f32[1,4096,256]{2,1,0:T(8,128)}, u32[]{:S(2)}) copy-start(f32[1,4096,256]{2,1,0:T(8,128)} %param.5) | copy-start | bytes 12582916
  52.7 46.4 %copy-start.1 = (f32[1,4096,256]{2,1,0:T(8,128)S(1)}, f32[1,4096,256]{2,1,0:T(8,128)}, u32[]{:S(2)}) copy-start(f32[1,4096,256]{2,1,0:T(8,128)} %param.5) | copy-start | bytes 12582916
  141.5 4.1 copy-start.4
  144.7 1.0 copy-start.6
  199.9 48.5 %copy-start.2 = (f32[1,4096,256]{2,1,0:T(8,128)S(1)}, f32[1,4096,256]{2,1,0:T(8,128)}, u32[]{:S(2)}) copy-start(f32[1,4096,256]{2,1,0:T(8,128)} %param.5) | copy-start | bytes 12582916
  278.5 1.6 copy-start.9
  293.4 3.6 copy-start.5
  293.4 3.6 copy-start.7
  350.6 47.9 %copy-start.3 = (f32[1,4096,256]{2,1,0:T(8,128)S(1)}, f32[1,4096,256]{2,1,0:T(8,128)}, u32[]{:S(2)}) copy-start(f32[1,4096,256]{2,1,0:T(8,128)} %param.5) | copy-start | bytes 12582916
  444.3 2.0 copy-start.10
  444.4 2.5 copy-start.8

commit v3 on v2

--- a/solution.py
+++ b/solution.py
@@ -145,9 +145,9 @@
         part_grad = jnp.einsum("rb,rk->bk", samples, res16, preferred_element_type=jnp.float32)
         own_solution = lax.dynamic_slice_in_dim(solution, offset, own_rows, 0)
         grad_own = exchange(part_grad, "row", 0, True, False) - ridge_weight * own_solution
-        term = jnp.dot(inverse, grad_own, precision=lax.Precision.HIGHEST)
+        term = jnp.dot(inverse, grad_own, precision=lax.Precision.HIGH)
         image = exchange(term, "row", 1, True, True)
-        update_own = jnp.einsum("bc,bk->ck", inverse, image, precision=lax.Precision.HIGHEST)
+        update_own = jnp.einsum("bc,bk->ck", inverse, image, precision=lax.Precision.HIGH)
         update = exchange(update_own, "row", 2, False, True)
         solution = solution + relaxation * update
         change = jnp.dot(samples, update.astype(jnp.bfloat16), preferred_element_type=jnp.float32)

time: 454 us -> 437 us (0.963)
  matrix products: 104 us -> 87.7 us
    dot_general x6, matrix products: 41.9 us -> 25.7 us  [the longest x3 15.4 us: run_group(): term = jnp.dot(inverse, grad_own, precision=lax.Precision.HIGH)]
where the time goes in v3:
time: 437 us; the launch traced here: 433 us
  Pallas kernels  321 us (73%)
  matrix products  87.7 us (20%)
  local copies, waits for them, and re-layouts  15 us (3%)
  other arithmetic  8.31 us (2%)
    pallas_call x12, Pallas kernels, exchange(): pl.pallas_call(functools.partial(exchange_kernel, axis, nbits, reduce, ga...  321 us
    dot_general x3, matrix products, run_group(): jnp.dot(samples, update.astype(jnp.bfloat16), preferred_element_type=jnp....  34.4 us
    dot_general x3, matrix products, run_group(): jnp.einsum('rb,rk->bk', samples, res16, preferred_element_type=jnp.float32)  27.6 us
    dot_general x3, matrix products, run_group(): term = jnp.dot(inverse, grad_own, precision=lax.Precision.HIGH)  15.4 us
    dot_general x3, matrix products, run_group(): jnp.einsum('bc,bk->ck', inverse, image, precision=lax.Precision.HIGH)  10.3 us

profile of v3, /device:TPU:0, one launch (start us, length us, event | category | flops | bytes accessed | tf_op | source)
XLA Modules:
  0.0 433.3 jit_solution(17723985882959389974)
XLA Ops:
  0.6 0.0 copy-start
  0.6 8.7 %fusion.20 = f32[4096,128]{1,0:T(8,128)S(1)} fusion(bf16[2048,4096]{1,0:T(8,128)(2,1)} %param.3, f32[2048,128]{1,0:T(8,128)} %param.4), kind=kOutput, calls=%fused_computation.33 | convolution fusion | flops 2147745792 | bytes 19922944 | tf_op jit(solution)/shard_map/rb,rk->bk/dot_general | solution.py:145
  9.3 35.2 %shard_map.50 = f32[256,128]{1,0:T(8,128)S(1)} custom-call(f32[2,2,2,2,256,128]{5,4,3,2,1,0:T(8,128)S(1)} %bitcast.84), custom_call_target="tpu_custom_call" | custom-call | tf_op jit(solution)/shard_map/pallas_call | solution.py:124
  44.5 0.0 copy-done
  44.5 3.7 convolution_bitcast_fusion.4
  48.2 2.1 copy.5
  50.3 0.0 copy-start.1
  50.3 46.8 %shard_map.51 = f32[2,2,2,2,256,128]{5,4,3,2,1,0:T(8,128)S(1)} custom-call(f32[2,2,2,2,256,128]{5,4,3,2,1,0:T(8,128)S(1)} %bitcast.88), custom_call_target="tpu_custom_call" | custom-call | tf_op jit(solution)/shard_map/pallas_call | solution.py:124
  97.2 0.0 copy-done.1
  97.2 3.4 fusion.9.x_ref
  100.6 22.4 %shard_map.52 = f32[2,2,2,2,256,128]{5,4,3,2,1,0:T(8,128)S(1)} custom-call(f32[256,128]{1,0:T(8,128)S(1)} %fusion.9.x_ref), custom_call_target="tpu_custom_call" | custom-call | tf_op jit(solution)/shard_map/pallas_call | solution.py:124
  123.0 1.7 broadcast_multiply_fusion.2
  124.7 11.5 %convolution_bitcast_fusion.7 = f32[2048,128]{0,1:T(8,128)S(1)} fusion(bf16[4096,128]{1,0:T(8,128)(2,1)S(1)} %bitcast.98, bf16[2048,4096]{1,0:T(8,128)(2,1)} %param.3), kind=kOutput, calls=%fused_computation.16 | convolution fusion | flops 2147483648 | bytes 18874368 | tf_op jit(solution)/shard_map/dot_general | solution.py:153
  136.1 0.3 copy.7
  136.5 0.0 copy-start.4
  136.5 3.1 shard_map.53
  139.6 0.1 broadcast_multiply_fusion.5
  139.6 0.0 copy-start.6
  139.7 1.0 copy-done.6
  140.6 0.0 copy-done.4
  140.6 0.1 bitcast_subtract_fusion.2
  140.7 9.5 %convolution_bitcast_fusion.1 = f32[4096,128]{0,1:T(8,128)} fusion(bf16[2048,4096]{1,0:T(8,128)(2,1)} %param.3, bf16[2048,128]{1,0:T(8,128)(2,1)S(1)} %bitcast_subtract_fusion.2), kind=kOutput, calls=%fused_computation.1 | convolution fusion | flops 2147483648 | bytes 19398656 | tf_op jit(solution)/shard_map/rb,rk->bk/dot_general | solution.py:145
  150.2 1.9 copy.8
  152.1 32.2 %shard_map.54 = f32[256,128]{1,0:T(8,128)S(1)} custom-call(f32[2,2,2,2,256,128]{5,4,3,2,1,0:T(8,128)S(1)} %bitcast.89), custom_call_target="tpu_custom_call" | custom-call | tf_op jit(solution)/shard_map/pallas_call | solution.py:124
  184.4 5.9 %convolution_bitcast_fusion.3 = f32[4096,128]{0,1:T(8,128)} fusion(f32[1,4096,256]{2,1,0:T(8,128)} %param.5, f32[256,128]{1,0:T(8,128)S(1)} %shard_map.54, f32[4096,128]{1,0:T(8,128)} %bitcast.96, s32[]{:T(128)S(6)} %select_n.4), kind=kOutput, calls=%fused_computation.3 | convolution fusion | flops 805371904 | bytes 6553604 | tf_op jit(solution)/shard_map/dot_general | solution.py:148
  190.2 2.3 copy.9
  192.6 0.0 copy-start.2
  192.6 48.3 %shard_map.55 = f32[2,2,2,2,256,128]{5,4,3,2,1,0:T(8,128)S(1)} custom-call(f32[2,2,2,2,256,128]{5,4,3,2,1,0:T(8,128)S(1)} %bitcast.90), custom_call_target="tpu_custom_call" | custom-call | tf_op jit(solution)/shard_map/pallas_call | solution.py:124
  240.8 0.0 copy-done.2
  240.9 3.4 fusion.12.x_ref
  244.3 22.9 %shard_map.56 = f32[2,2,2,2,256,128]{5,4,3,2,1,0:T(8,128)S(1)} custom-call(f32[256,128]{1,0:T(8,128)S(1)} %fusion.12.x_ref), custom_call_target="tpu_custom_call" | custom-call | tf_op jit(solution)/shard_map/pallas_call | solution.py:124
  267.2 0.0 copy-start.9
  267.2 0.3 fusion.35
  267.5 1.2 copy-done.9
  268.8 1.5 bitcast_add_fusion.1
  270.3 11.5 %convolution_bitcast_fusion.6 = f32[2048,128]{0,1:T(8,128)S(1)} fusion(bf16[4096,128]{1,0:T(8,128)(2,1)S(1)} %bitcast.97, bf16[2048,4096]{1,0:T(8,128)(2,1)} %param.3), kind=kOutput, calls=%fused_computation.15 | convolution fusion | flops 2147483648 | bytes 18874368 | tf_op jit(solution)/shard_map/dot_general | solution.py:153
  281.8 0.3 copy.11
  282.1 0.0 copy-start.5
  282.1 0.0 copy-start.7
  282.1 3.1 shard_map.57
  285.2 0.1 broadcast_multiply_fusion.4
  285.3 0.0 copy-done.5
  285.3 0.0 copy-done.7
  285.3 0.2 bitcast_subtract_fusion.1
  285.5 9.5 %convolution_bitcast_fusion = f32[4096,128]{0,1:T(8,128)} fusion(bf16[2048,4096]{1,0:T(8,128)(2,1)} %param.3, f32[2048,128]{1,0:T(8,128)S(1)} %bitcast_subtract_fusion.1), kind=kOutput, calls=%fused_computation | convolution fusion | flops 2147745792 | bytes 19922944 | tf_op jit(solution)/shard_map/rb,rk->bk/dot_general | solution.py:145
  295.0 2.1 copy.12
  297.1 32.5 %shard_map.58 = f32[256,128]{1,0:T(8,128)S(1)} custom-call(f32[2,2,2,2,256,128]{5,4,3,2,1,0:T(8,128)S(1)} %bitcast.91), custom_call_target="tpu_custom_call" | custom-call | tf_op jit(solution)/shard_map/pallas_call | solution.py:124
  329.6 5.9 %convolution_bitcast_fusion.2 = f32[4096,128]{0,1:T(8,128)} fusion(f32[1,4096,256]{2,1,0:T(8,128)} %param.5, f32[256,128]{1,0:T(8,128)S(1)} %shard_map.58, f32[4096,128]{1,0:T(8,128)} %bitcast_add_fusion.1, s32[]{:T(128)S(6)} %select_n.4), kind=kOutput, calls=%fused_computation.2 | convolution fusion | flops 805371904 | bytes 6553604 | tf_op jit(solution)/shard_map/dot_general | solution.py:148
  335.4 1.9 copy.13
  337.3 0.0 copy-start.3
  337.3 48.7 %shard_map.59 = f32[2,2,2,2,256,128]{5,4,3,2,1,0:T(8,128)S(1)} custom-call(f32[2,2,2,2,256,128]{5,4,3,2,1,0:T(8,128)S(1)} %bitcast.92), custom_call_target="tpu_custom_call" | custom-call | tf_op jit(solution)/shard_map/pallas_call | solution.py:124
  386.1 0.0 copy-done.3
  386.1 3.4 fusion.15.x_ref
  389.5 22.9 %shard_map.60 = f32[2,2,2,2,256,128]{5,4,3,2,1,0:T(8,128)S(1)} custom-call(f32[256,128]{1,0:T(8,128)S(1)} %fusion.15.x_ref), custom_call_target="tpu_custom_call" | custom-call | tf_op jit(solution)/shard_map/pallas_call | solution.py:124
  412.4 1.7 fusion.34
  414.1 11.5 %convolution_bitcast_fusion.5 = f32[2048,128]{0,1:T(8,128)S(1)} fusion(bf16[4096,128]{1,0:T(8,128)(2,1)S(1)} %bitcast.99, bf16[2048,4096]{1,0:T(8,128)(2,1)} %param.3), kind=kOutput, calls=%fused_computation.14 | convolution fusion | flops 2147483648 | bytes 18874368 | tf_op jit(solution)/shard_map/dot_general | solution.py:153
  425.6 0.3 copy.15
  425.9 3.1 shard_map.61
  429.0 0.1 broadcast_multiply_fusion.3
  429.1 0.0 copy-start.8
  429.1 1.1 bitcast_subtract_fusion
  430.1 0.8 copy-done.10
  430.9 0.7 copy-done.8
  431.6 1.5 bitcast_add_fusion
  (1 shorter events, 0.0 us)
Async XLA Ops:
  0.6 43.9 %copy-start = (f32[1,4096,256]{2,1,0:T(8,128)S(1)}, f32[1,4096,256]{2,1,0:T(8,128)}, u32[]{:S(2)}) copy-start(f32[1,4096,256]{2,1,0:T(8,128)} %param.5) | copy-start | bytes 12582916
  50.3 46.8 %copy-start.1 = (f32[1,4096,256]{2,1,0:T(8,128)S(1)}, f32[1,4096,256]{2,1,0:T(8,128)}, u32[]{:S(2)}) copy-start(f32[1,4096,256]{2,1,0:T(8,128)} %param.5) | copy-start | bytes 12582916
  136.5 4.1 copy-start.4
  139.6 1.0 copy-start.6
  192.6 48.3 %copy-start.2 = (f32[1,4096,256]{2,1,0:T(8,128)S(1)}, f32[1,4096,256]{2,1,0:T(8,128)}, u32[]{:S(2)}) copy-start(f32[1,4096,256]{2,1,0:T(8,128)} %param.5) | copy-start | bytes 12582916
  267.2 1.6 copy-start.9
  282.1 3.2 copy-start.5
  282.1 3.2 copy-start.7
  337.3 48.8 %copy-start.3 = (f32[1,4096,256]{2,1,0:T(8,128)S(1)}, f32[1,4096,256]{2,1,0:T(8,128)}, u32[]{:S(2)}) copy-start(f32[1,4096,256]{2,1,0:T(8,128)} %param.5) | copy-start | bytes 12582916
  429.0 2.0 copy-start.10
  429.1 2.5 copy-start.8

commit v4 on v3

--- a/solution.py
+++ b/solution.py
@@ -138,14 +138,66 @@
     return out.reshape(-1, width)
 
 
+def gradient_kernel(res_ref, samples_ref, out_ref):
+    out_ref[...] = jnp.dot(
+        res_ref[...], samples_ref[...], preferred_element_type=jnp.float32
+    ).T
+
+
+def gradient(samples, res16):
+    rows, features = samples.shape
+    width = res16.shape[1]
+    tile = min(512, features)
+    return pl.pallas_call(
+        gradient_kernel,
+        grid=(features // tile,),
+        out_shape=jax.ShapeDtypeStruct((features, width), jnp.float32),
+        in_specs=[
+            pl.BlockSpec((width, rows), lambda i: (0, 0)),
+            pl.BlockSpec((rows, tile), lambda i: (0, i)),
+        ],
+        out_specs=pl.BlockSpec((tile, width), lambda i: (i, 0)),
+        compiler_params=pltpu.CompilerParams(vmem_limit_bytes=24 << 20),
+    )(res16.T, samples)
+
+
+def halves(x):
+    high = x.astype(jnp.bfloat16)
+    return high, (x - high.astype(jnp.float32)).astype(jnp.bfloat16)
+
+
+def term_kernel(inverse_ref, grad_ref, out_ref):
+    w_high, w_low = halves(inverse_ref[...])
+    g_high, g_low = halves(grad_ref[...])
+    dot = functools.partial(jnp.dot, preferred_element_type=jnp.float32)
+    out_ref[...] = dot(w_high, g_low) + dot(w_low, g_high) + dot(w_high, g_high)
+
+
+def factor_term(inverse, grad):
+    features, own_rows = inverse.shape
+    width = grad.shape[1]
+    tile = min(512, features)
+    return pl.pallas_call(
+        term_kernel,
+        grid=(features // tile,),
+        out_shape=jax.ShapeDtypeStruct((features, width), jnp.float32),
+        in_specs=[
+            pl.BlockSpec((tile, own_rows), lambda i: (i, 0)),
+            pl.BlockSpec((own_rows, width), lambda i: (0, 0)),
+        ],
+        out_specs=pl.BlockSpec((tile, width), lambda i: (i, 0)),
+        compiler_params=pltpu.CompilerParams(vmem_limit_bytes=24 << 20),
+    )(inverse, grad)
+
+
 def run_group(samples, residual, inverse, own_rows, offset, relaxation):
     solution = jnp.zeros((samples.shape[1], residual.shape[1]), jnp.float32)
     for sweep in range(ROUNDS):
         res16 = residual.astype(jnp.bfloat16)
-        part_grad = jnp.einsum("rb,rk->bk", samples, res16, preferred_element_type=jnp.float32)
+        part_grad = gradient(samples, res16)
         own_solution = lax.dynamic_slice_in_dim(solution, offset, own_rows, 0)
         grad_own = exchange(part_grad, "row", 0, True, False) - ridge_weight * own_solution
-        term = jnp.dot(inverse, grad_own, precision=lax.Precision.HIGH)
+        term = factor_term(inverse, grad_own)
         image = exchange(term, "row", 1, True, True)
         update_own = jnp.einsum("bc,bk->ck", inverse, image, precision=lax.Precision.HIGH)
         update = exchange(update_own, "row", 2, False, True)

time: 437 us -> 438 us (level)
  matrix products: 87.7 us -> 45.7 us
  Pallas kernels: 321 us -> 348 us
  local copies, waits for them, and re-layouts: 15 us -> 28.7 us
  other arithmetic: 8.31 us -> 14.1 us
    dot_general x6 -> x0, matrix products: 43 us -> none  [the longest x3 27.6 us: run_group(): jnp.einsum('rb,rk->bk', samples, res16, preferred_element_type=jnp.float32)]
    pallas_call x0 -> x6, Pallas kernels: none -> 27 us  [the longest x3 17.4 us: gradient(): pl.pallas_call(gradient_kernel, grid=(features // tile,), out_shape=jax.S...]
    unnamed x22 -> x20, local copies, waits for them, and re-layouts: 3.71 us -> 23.3 us
    dot_general x5 -> x0, local copies, waits for them, and re-layouts: 10.3 us -> none  [the longest x3 6.3 us: run_group(): term = jnp.dot(inverse, grad_own, precision=lax.Precision.HIGH)]
where the time goes in v4:
time: 438 us
  Pallas kernels  348 us (79%)
  matrix products  45.7 us (10%)
  local copies, waits for them, and re-layouts  28.7 us (7%)
  other arithmetic  14.1 us (3%)
    pallas_call x12, Pallas kernels, exchange(): pl.pallas_call(functools.partial(exchange_kernel, axis, nbits, reduce, ga...  321 us
    dot_general x3, matrix products, run_group(): jnp.dot(samples, update.astype(jnp.bfloat16), preferred_element_type=jnp....  35.4 us
    unnamed x20, local copies, waits for them, and re-layouts  23.3 us
    pallas_call x3, Pallas kernels, gradient(): pl.pallas_call(gradient_kernel, grid=(features // tile,), out_shape=jax.S...  17.4 us
    dot_general x3, matrix products, run_group(): jnp.einsum('bc,bk->ck', inverse, image, precision=lax.Precision.HIGH)  10.3 us
    pallas_call x3, Pallas kernels, factor_term(): pl.pallas_call(term_kernel, grid=(features // tile,), out_shape=jax.Shape...  9.58 us

profile of v4, /device:TPU:0, one launch (start us, length us, event | category | flops | bytes accessed | tf_op | source)
XLA Modules:
  0.0 437.6 jit_solution(2048760277670198485)
XLA Ops:
  0.6 1.6 copy.5
  2.2 0.1 convert_bitcast_fusion.2.res_ref
  2.3 0.0 copy-start
  2.3 5.8 %copy-done = bf16[2048,4096]{1,0:T(8,128)(2,1)S(1)} copy-done((bf16[2048,4096]{1,0:T(8,128)(2,1)S(1)}, bf16[2048,4096]{1,0:T(8,128)(2,1)}, u32[]{:S(2)}) %copy-start) | copy-done | bytes 16777240
  8.0 0.0 copy-start.3
  8.0 5.8 %shard_map.50 = f32[4096,128]{1,0:T(8,128)S(1)} custom-call(bf16[128,2048]{1,0:T(8,128)(2,1)S(1)} %convert_bitcast_fusion.2.res_ref, bf16[2048,4096]{1,0:T(8,128)(2,1)S(1)} %copy-done), custom_call_target="tpu_custom_call" | custom-call | tf_op jit(solution)/shard_map/pallas_call | solution.py:151
  13.9 35.2 %shard_map.51.grad_ref = f32[256,128]{1,0:T(8,128)S(1)} custom-call(f32[2,2,2,2,256,128]{5,4,3,2,1,0:T(8,128)S(1)} %bitcast.61), custom_call_target="tpu_custom_call" | custom-call | tf_op jit(solution)/shard_map/pallas_call | solution.py:124
  49.1 0.0 copy-done.3
  49.1 3.1 shard_map.52
  52.2 47.0 %shard_map.53 = f32[2,2,2,2,256,128]{5,4,3,2,1,0:T(8,128)S(1)} custom-call(f32[2,2,2,2,256,128]{5,4,3,2,1,0:T(8,128)S(1)} %bitcast.62), custom_call_target="tpu_custom_call" | custom-call | tf_op jit(solution)/shard_map/pallas_call | solution.py:124
  99.2 3.4 convolution_bitcast_fusion.5.x_ref
  102.6 22.3 %shard_map.54 = f32[2,2,2,2,256,128]{5,4,3,2,1,0:T(8,128)S(1)} custom-call(f32[256,128]{1,0:T(8,128)S(1)} %convolution_bitcast_fusion.5.x_ref), custom_call_target="tpu_custom_call" | custom-call | tf_op jit(solution)/shard_map/pallas_call | solution.py:124
  124.9 1.7 broadcast_multiply_fusion.2
  126.5 11.5 %convolution_bitcast_fusion.2 = f32[2048,128]{0,1:T(8,128)S(1)} fusion(bf16[4096,128]{1,0:T(8,128)(2,1)S(1)} %bitcast.74, bf16[2048,4096]{1,0:T(8,128)(2,1)} %samples_ref.5), kind=kOutput, calls=%fused_computation.2 | convolution fusion | flops 2147483648 | bytes 18874368 | tf_op jit(solution)/shard_map/dot_general | solution.py:205
  138.0 0.3 copy.7
  138.3 3.1 shard_map.55
  141.4 0.1 broadcast_multiply_fusion.5
  141.5 0.3 copy.9
  141.8 0.2 convert_bitcast_fusion.1
  142.0 0.0 copy-start.1
  142.0 5.8 %copy-done.1 = bf16[2048,4096]{1,0:T(8,128)(2,1)S(1)} copy-done((bf16[2048,4096]{1,0:T(8,128)(2,1)S(1)}, bf16[2048,4096]{1,0:T(8,128)(2,1)}, u32[]{:S(2)}) %copy-start.1) | copy-done | bytes 16777240
  147.8 0.0 copy-start.4
  147.8 5.8 %shard_map.56 = f32[4096,128]{1,0:T(8,128)S(1)} custom-call(bf16[128,2048]{1,0:T(8,128)(2,1)S(1)} %get-tuple-element.6.res_ref, bf16[2048,4096]{1,0:T(8,128)(2,1)S(1)} %copy-done.1), custom_call_target="tpu_custom_call" | custom-call | tf_op jit(solution)/shard_map/pallas_call | solution.py:151
  153.6 32.2 %shard_map.57 = f32[256,128]{1,0:T(8,128)S(1)} custom-call(f32[2,2,2,2,256,128]{5,4,3,2,1,0:T(8,128)S(1)} %bitcast.64), custom_call_target="tpu_custom_call" | custom-call | tf_op jit(solution)/shard_map/pallas_call | solution.py:124
  185.8 0.9 multiply_subtract_fusion.1.grad_ref
  186.7 0.0 copy-done.4
  186.8 3.2 shard_map.58
  190.0 48.5 %shard_map.59 = f32[2,2,2,2,256,128]{5,4,3,2,1,0:T(8,128)S(1)} custom-call(f32[2,2,2,2,256,128]{5,4,3,2,1,0:T(8,128)S(1)} %bitcast.65), custom_call_target="tpu_custom_call" | custom-call | tf_op jit(solution)/shard_map/pallas_call | solution.py:124
  238.6 3.4 convolution_bitcast_fusion.4.x_ref
  242.0 22.4 %shard_map.60 = f32[2,2,2,2,256,128]{5,4,3,2,1,0:T(8,128)S(1)} custom-call(f32[256,128]{1,0:T(8,128)S(1)} %convolution_bitcast_fusion.4.x_ref), custom_call_target="tpu_custom_call" | custom-call | tf_op jit(solution)/shard_map/pallas_call | solution.py:124
  264.4 1.7 fusion.4
  266.0 11.5 %convolution_bitcast_fusion.1 = f32[2048,128]{0,1:T(8,128)S(1)} fusion(bf16[4096,128]{1,0:T(8,128)(2,1)S(1)} %bitcast.75, bf16[2048,4096]{1,0:T(8,128)(2,1)} %samples_ref.5), kind=kOutput, calls=%fused_computation.1 | convolution fusion | flops 2147483648 | bytes 18874368 | tf_op jit(solution)/shard_map/dot_general | solution.py:205
  277.5 0.3 copy.11
  277.9 3.1 shard_map.61
  280.9 0.1 broadcast_multiply_fusion.4
  281.0 0.3 copy.12
  281.3 1.1 convert_bitcast_fusion
  282.5 0.0 copy-start.2
  282.5 5.8 %copy-done.2 = bf16[2048,4096]{1,0:T(8,128)(2,1)S(1)} copy-done((bf16[2048,4096]{1,0:T(8,128)(2,1)S(1)}, bf16[2048,4096]{1,0:T(8,128)(2,1)}, u32[]{:S(2)}) %copy-start.2) | copy-done | bytes 16777240
  288.2 0.0 copy-start.7
  288.2 5.8 %shard_map.62 = f32[4096,128]{1,0:T(8,128)S(1)} custom-call(bf16[128,2048]{1,0:T(8,128)(2,1)S(1)} %get-tuple-element.4.res_ref, bf16[2048,4096]{1,0:T(8,128)(2,1)S(1)} %copy-done.2), custom_call_target="tpu_custom_call" | custom-call | tf_op jit(solution)/shard_map/pallas_call | solution.py:151
  294.1 0.0 copy-start.6
  294.1 33.0 %shard_map.63 = f32[256,128]{1,0:T(8,128)S(1)} custom-call(f32[2,2,2,2,256,128]{5,4,3,2,1,0:T(8,128)S(1)} %bitcast.67), custom_call_target="tpu_custom_call" | custom-call | tf_op jit(solution)/shard_map/pallas_call | solution.py:124
  327.0 0.0 copy-done.7
  327.0 0.0 copy-done.6
  327.0 0.0 copy-start.5
  327.1 0.2 bitcast_add_fusion.1
  327.3 1.9 copy-done.5
  329.2 3.3 shard_map.64
  332.5 48.4 %shard_map.65 = f32[2,2,2,2,256,128]{5,4,3,2,1,0:T(8,128)S(1)} custom-call(f32[2,2,2,2,256,128]{5,4,3,2,1,0:T(8,128)S(1)} %bitcast.68), custom_call_target="tpu_custom_call" | custom-call | tf_op jit(solution)/shard_map/pallas_call | solution.py:124
  380.9 3.4 convolution_bitcast_fusion.3.x_ref
  384.3 23.0 %shard_map.66 = f32[2,2,2,2,256,128]{5,4,3,2,1,0:T(8,128)S(1)} custom-call(f32[256,128]{1,0:T(8,128)S(1)} %convolution_bitcast_fusion.3.x_ref), custom_call_target="tpu_custom_call" | custom-call | tf_op jit(solution)/shard_map/pallas_call | solution.py:124
  407.3 1.7 fusion.3
  409.0 12.4 %convolution_bitcast_fusion = f32[2048,128]{0,1:T(8,128)} fusion(bf16[4096,128]{1,0:T(8,128)(2,1)S(1)} %bitcast.76, bf16[2048,4096]{1,0:T(8,128)(2,1)} %samples_ref.5), kind=kOutput, calls=%fused_computation | convolution fusion | flops 2147483648 | bytes 18874368 | tf_op jit(solution)/shard_map/dot_general | solution.py:205
  421.4 1.5 copy.14
  423.0 3.1 shard_map.67
  426.1 0.0 copy-start.8
  426.1 1.0 broadcast_multiply_fusion.3
  427.1 2.5 copy.15
  429.6 0.0 copy-done.8
  429.6 2.3 sub.19
  431.9 2.5 copy.16
  434.5 3.1 bitcast_add_fusion
  (1 shorter events, 0.0 us)
Async XLA Ops:
  2.3 5.8 %copy-start = (bf16[2048,4096]{1,0:T(8,128)(2,1)S(1)}, bf16[2048,4096]{1,0:T(8,128)(2,1)}, u32[]{:S(2)}) copy-start(bf16[2048,4096]{1,0:T(8,128)(2,1)} %samples_ref.5) | copy-start | bytes 50331652
  8.0 41.1 %copy-start.3 = (f32[1,4096,256]{2,1,0:T(8,128)S(1)}, f32[1,4096,256]{2,1,0:T(8,128)}, u32[]{:S(2)}) copy-start(f32[1,4096,256]{2,1,0:T(8,128)} %param.5) | copy-start | bytes 12582916
  142.0 5.8 %copy-start.1 = (bf16[2048,4096]{1,0:T(8,128)(2,1)S(1)}, bf16[2048,4096]{1,0:T(8,128)(2,1)}, u32[]{:S(2)}) copy-start(bf16[2048,4096]{1,0:T(8,128)(2,1)} %samples_ref.5) | copy-start | bytes 50331652
  147.8 39.0 %copy-start.4 = (f32[1,4096,256]{2,1,0:T(8,128)S(1)}, f32[1,4096,256]{2,1,0:T(8,128)}, u32[]{:S(2)}) copy-start(f32[1,4096,256]{2,1,0:T(8,128)} %param.5) | copy-start | bytes 12582916
  282.5 5.8 %copy-start.2 = (bf16[2048,4096]{1,0:T(8,128)(2,1)S(1)}, bf16[2048,4096]{1,0:T(8,128)(2,1)}, u32[]{:S(2)}) copy-start(bf16[2048,4096]{1,0:T(8,128)(2,1)} %samples_ref.5) | copy-start | bytes 50331652
  288.2 38.8 %copy-start.7 = (f32[2,2,2,2,256,128]{5,4,3,2,1,0:T(8,128)S(1)}, f32[2,2,2,2,256,128]{5,4,3,2,1,0:T(8,128)}, u32[]{:S(2)}) copy-start(f32[2,2,2,2,256,128]{5,4,3,2,1,0:T(8,128)} %get-tuple-element.11) | copy-start | bytes 6291460
  294.1 33.0 %copy-start.6 = (f32[2,2,2,2,256,128]{5,4,3,2,1,0:T(8,128)S(1)}, f32[2,2,2,2,256,128]{5,4,3,2,1,0:T(8,128)}, u32[]{:S(2)}) copy-start(f32[2,2,2,2,256,128]{5,4,3,2,1,0:T(8,128)} %get-tuple-element.12) | copy-start | bytes 6291460
  327.0 2.2 copy-start.5
  426.1 3.6 copy-start.8
